TPU v7x, 256 devices: a whole 4x4x8 slice. The times are simulated.
256 devices in a mesh: seq: 64 (over z, y, core), tp: 4 (over x).
Axes of the slice: x: 4, y: 4, z: 8, core: 2. Of those that a mesh axis runs over, the one named last changes fastest.
Arguments:
- db_tokens: int32 [32768, 128], P('seq'), may hold values from 0 to 16383
- db_parent: int32 [32768, 128], P('seq'), may hold values from 0 to 126, as said below
- db_depth: int32 [32768, 128], P('seq'), may hold values from 0 to 31, as said below
- nb_rows: int32 [512, 2], P('seq'), may hold values from 0 to 32767, as said below
- seq_start: int32 [512], P('seq'), may hold values 0 or 1
- table: bfloat16 [16384, 1024], P(None, 'tp'), may hold values from -40 to 40
- depth_table: bfloat16 [32, 1024], P(None, 'tp'), may hold values from -3 to 3
- enc_gain: float32 [1024], replicated, may hold values from 0.25 to 1.75
- enc_qkv: bfloat16 [1024, 3, 1024], P('seq', None, 'tp'), may hold values from -0.1875 to 0.1875
- tree_bias: float32 [8], replicated, may hold values from 1 to 4
- enc_wo: bfloat16 [1024, 1024], P('tp', 'seq'), may hold values from -0.1875 to 0.1875
- cond_kv: bfloat16 [32768, 2, 1024], P('seq', None, 'tp'), may hold values from -150 to 150
- queries: bfloat16 [32768, 4096], P('seq', 'tp'), may hold values from -150 to 150
- cca_kv: bfloat16 [1024, 2, 512], P('seq', None, 'tp'), may hold values from -0.1875 to 0.1875
Outputs:
- attended: bfloat16 [32768, 4096], P('seq', 'tp')
Inputs may be any that keep to these rules, and one draw needn't show every extreme that they name: `db_parent`: position 0 of every stored neighbour is its own parent; every other position's parent is one of the three positions just before it. `db_depth`: position 0 has depth 0; every other position has its parent's depth plus one, capped at 31. `nb_rows`: rows 512 * i to 512 * (i + 1) - 1 of the database lie on index i of seq. Of the 16 neighbours of one index's blocks at most 1 lie on any one index; at most 32 neighbours of all blocks lie on one index, and in every draw some index holds exactly 32.
All inputs are finite; a program needn't handle non-finite values. No bound on the sum of `seq_start` on one device may be relied on, other than what follows from the above.
Results may differ from a plain program's by a relative error of at most 0.0223.
The roundings to bfloat16 on the way count: a program that leaves them out, or rounds other values in their place, can miss the bound.
Values may be sent and summed in bfloat16 or wider, within the bound.
No kernel may reach another device: no remote copies, remote signals or barrier semaphores. Data moves between devices by JAX's collectives and lax.ppermute only.
A program may use at most 128 MiB of HBM per device.

v0:
```python
import math
import jax
import jax.numpy as jnp
from jax import lax
from jax.sharding import PartitionSpec as P

HD = 128


def from_behind(value, axis, steps):
    count = lax.axis_size(axis)
    initial, last = (max(0, -steps), min(count, count - steps))
    return lax.ppermute(value, axis, [(source, source + steps) for source in range(initial, last)])


def normalize(embedded, gain):
    embedded_f = embedded.astype(jnp.float32)
    return (
        embedded_f
        * lax.rsqrt(jnp.mean(embedded_f * embedded_f, axis=-1, keepdims=True) + 1e-05)
        * gain
    ).astype(jnp.bfloat16)


def encoder_mix(normed, parents, conditioning, w_qkv, bias, head_count):
    unit_count = normed.shape[0]
    length = normed.shape[1]
    blocks = conditioning.shape[0]
    pair_count = unit_count // blocks
    cond_len = conditioning.shape[1]
    score_scale = 1.0 / math.sqrt(HD)
    projected = jnp.einsum(
        "une,eaf->unaf", normed, w_qkv, preferred_element_type=jnp.float32
    ).astype(jnp.bfloat16)
    shaped = projected.reshape(blocks, pair_count, length, 3, head_count, HD)
    query_part = shaped[:, :, :, 0]
    key_part = shaped[:, :, :, 1]
    value_part = shaped[:, :, :, 2]
    cond_keys = conditioning[:, :, 0].reshape(blocks, cond_len, head_count, HD)
    cond_values = conditioning[:, :, 1].reshape(blocks, cond_len, head_count, HD)
    self_scores = (
        jnp.einsum("cpihd,cpjhd->cphij", query_part, key_part, preferred_element_type=jnp.float32)
        * score_scale
    )
    parent_hit = (
        parents.reshape(blocks, pair_count, length)[:, :, :, None]
        == jnp.arange(length, dtype=jnp.float32)[None, None, None, :]
    ).astype(jnp.float32)
    self_scores = self_scores + bias[None, None, :, None, None] * parent_hit[:, :, None]
    cond_scores = (
        jnp.einsum("cpihd,crhd->cphir", query_part, cond_keys, preferred_element_type=jnp.float32)
        * score_scale
    )
    weights = jax.nn.softmax(jnp.concatenate([self_scores, cond_scores], axis=-1), axis=-1).astype(
        jnp.bfloat16
    )
    mixed = jnp.einsum(
        "cphij,cpjhd->cpihd", weights[..., :length], value_part, preferred_element_type=jnp.float32
    )
    mixed = mixed + jnp.einsum(
        "cphir,crhd->cpihd", weights[..., length:], cond_values, preferred_element_type=jnp.float32
    )
    return mixed.astype(jnp.bfloat16).reshape(unit_count, length, head_count * HD)


def attend(query, key_value):
    blocks, key_rows = (key_value.shape[0], key_value.shape[1])
    token_count = query.shape[1]
    head_count = query.shape[2]
    kv_heads = key_value.shape[3] // HD
    group = head_count // kv_heads
    grouped = query.reshape(blocks, token_count, kv_heads, group, HD)
    key_part = key_value[:, :, 0].reshape(blocks, key_rows, kv_heads, HD)
    value_part = key_value[:, :, 1].reshape(blocks, key_rows, kv_heads, HD)
    scores = jnp.einsum(
        "ctkgd,cpkd->ckgtp", grouped, key_part, preferred_element_type=jnp.float32
    ) * (1.0 / math.sqrt(HD))
    weights = jax.nn.softmax(scores, axis=-1).astype(jnp.bfloat16)
    output = jnp.einsum(
        "ckgtp,cpkd->ctkgd", weights, value_part, preferred_element_type=jnp.float32
    ).astype(jnp.bfloat16)
    return output.reshape(blocks, token_count, head_count, HD)


def shards(
    db_tokens,
    db_parent,
    db_depth,
    nb_rows,
    seq_start,
    table,
    depth_table,
    enc_gain,
    enc_qkv,
    tree_bias,
    enc_wo,
    cond_kv,
    queries,
    cca_kv,
):
    seq_size = lax.axis_size("seq")
    tp_size = lax.axis_size("tp")
    block_count, pair_count = nb_rows.shape
    unit_count = block_count * pair_count
    stored = db_tokens.shape[0]
    length = db_tokens.shape[1]
    slot_count = max(1, 2 * unit_count // seq_size)
    flat_rows = nb_rows.reshape(unit_count)
    holder = flat_rows // stored
    local_row = flat_rows % stored
    ordering = jnp.arange(unit_count, dtype=jnp.int32)
    earlier = jnp.sum(
        ((holder[:, None] == holder[None, :]) & (ordering[:, None] > ordering[None, :])).astype(
            jnp.int32
        ),
        axis=1,
    )
    target = holder * slot_count + earlier
    places = jnp.arange(seq_size * slot_count, dtype=jnp.int32)
    request = jnp.sum(
        jnp.where(target[None, :] == places[:, None], local_row[None, :], 0), axis=1
    ).reshape(seq_size, slot_count)
    wanted = lax.all_to_all(request, "seq", split_axis=0, concat_axis=0, tiled=True)
    tokens = jnp.take(db_tokens, wanted, axis=0)
    depths = jnp.take(db_depth, wanted, axis=0)
    parents = jnp.take(db_parent, wanted, axis=0).astype(jnp.bfloat16)
    embedded = (
        jnp.take(table, tokens, axis=0).astype(jnp.float32)
        + jnp.take(depth_table, depths, axis=0).astype(jnp.float32)
    ).astype(jnp.bfloat16)
    fetched = lax.all_to_all(embedded, "seq", split_axis=0, concat_axis=0, tiled=True)
    fetched_parents = lax.all_to_all(parents, "seq", split_axis=0, concat_axis=0, tiled=True)
    embedded = jnp.take(
        fetched.reshape((seq_size * slot_count,) + fetched.shape[2:]), target, axis=0
    )
    parents = jnp.take(
        fetched_parents.reshape(seq_size * slot_count, length), target, axis=0
    ).astype(jnp.float32)
    row_qkv, row_out = (
        lax.all_gather(enc_qkv, "seq", axis=0, tiled=True),
        lax.all_gather(enc_wo, "seq", axis=1, tiled=True),
    )
    cond_columns = cond_kv.shape[2]
    cond_len = cond_kv.shape[0] // block_count
    full_width = row_qkv.shape[0]
    head_count = row_qkv.shape[2] // HD
    conditioning = cond_kv.reshape(block_count, cond_len, 2, cond_columns)
    gathered = lax.all_gather(embedded, "tp", axis=2, tiled=True)
    normed = normalize(gathered, enc_gain)
    bias_here = lax.dynamic_slice_in_dim(tree_bias, lax.axis_index("tp") * head_count, head_count)
    mixed = encoder_mix(normed, parents, conditioning, row_qkv, bias_here, head_count).reshape(
        unit_count * length, head_count * HD
    )
    row_share = unit_count * length // tp_size
    increment = lax.psum_scatter(
        jnp.dot(mixed, row_out, preferred_element_type=jnp.float32),
        "tp",
        scatter_dimension=0,
        tiled=True,
    )
    residual = lax.dynamic_slice_in_dim(
        gathered.reshape(unit_count * length, full_width),
        lax.axis_index("tp") * row_share,
        row_share,
        0,
    )
    encoded_part = (residual.astype(jnp.float32) + increment).astype(jnp.bfloat16)
    encoded = lax.all_gather(encoded_part, "tp", axis=0, tiled=True)
    kv_weight = lax.all_gather(cca_kv, "seq", axis=0, tiled=True)
    key_rows = pair_count * length
    keys_values = jnp.einsum(
        "re,eaf->raf", encoded, kv_weight, preferred_element_type=jnp.float32
    ).astype(jnp.bfloat16)
    keys_values = keys_values.reshape(block_count, key_rows, 2, keys_values.shape[2])
    carried = from_behind(keys_values[block_count - 1], "seq", 1)
    previous = jnp.concatenate([carried[None], keys_values[: block_count - 1]], axis=0)
    head_queries = queries.shape[1] // HD
    query_heads = queries.reshape(block_count, cond_len, head_queries, HD)
    leading = attend(query_heads[:, : cond_len - 1], previous)
    trailing = attend(query_heads[:, cond_len - 1 :], keys_values)
    block_index = lax.axis_index("seq") * block_count + jnp.arange(block_count, dtype=jnp.int32)
    allowed = (block_index > 0) & (seq_start == 0)
    leading = jnp.where(allowed[:, None, None, None], leading, jnp.zeros_like(leading))
    attended = jnp.concatenate([leading, trailing], axis=1)
    return attended.reshape(block_count * cond_len, head_queries * HD)


def solution(mesh):
    in_specs = (
        P("seq", None),
        P("seq", None),
        P("seq", None),
        P("seq", None),
        P("seq"),
        P(None, "tp"),
        P(None, "tp"),
        P(),
        P("seq", None, "tp"),
        P(),
        P("tp", "seq"),
        P("seq", None, "tp"),
        P("seq", "tp"),
        P("seq", None, "tp"),
    )
    out_specs = P("seq", "tp")
    return jax.shard_map(shards, mesh=mesh, in_specs=in_specs, out_specs=out_specs, check_vma=False)
```

profile of v0, /device:TPU:128, one launch (start us, length us, event | category | flops | bytes accessed | tf_op | source)
XLA Modules:
  0.0 528.6 jit_solution(15645028171673913726)
XLA Ops:
  7.8 15.1 %all_to_all.22 = s32[64,1,1]{2,1,0:T(1,128)S(1)} all-to-all(s32[64,1,1]{2,1,0:T(1,128)S(1)} %copy.110), channel_id=1, replica_groups=mesh['seq'=64,'tp'=4] {'seq'}, dimensions={0} | all-to-all | bytes 512 | tf_op jit(solution)/shard_map/all_to_all | solution.py:123
  26.6 33.1 %gather_fusion.1 = bf16[8192,256]{1,0:T(8,128)(2,1)} fusion(bf16[32,256]{1,0:T(8,128)(2,1)S(1)} %copy-done.2, s32[8192]{0:T(1024)S(1)} %get-tuple-element.16), kind=kCustom, calls=%fused_computation.4 | custom fusion | bytes 8421376 | tf_op jit(solution)/shard_map/jit(_take)/gather | solution.py:129
  59.7 35.5 %gather_fusion = bf16[8192,256]{1,0:T(8,128)(2,1)} fusion(bf16[16384,256]{1,0:T(8,128)(2,1)} %param.21, s32[8192]{0:T(1024)S(1)} %get-tuple-element.15), kind=kCustom, calls=%fused_computation.3 | custom fusion | bytes 8421376 | tf_op jit(solution)/shard_map/jit(_take)/gather | solution.py:128
  95.2 8.5 %add_convert_fusion = bf16[64,1,128,256]{3,2,1,0:T(8,128)(2,1)} fusion(bf16[64,1,128,256]{3,2,1,0:T(8,128)(2,1)} %bitcast.204, bf16[64,1,128,256]{3,2,1,0:T(8,128)(2,1)} %bitcast.205, pred[64,128]{1,0:T(8,128)(4,1)S(1)} %get-tuple-element.14, pred[64,128]{1,0:T(8,128)(4,1)S(1)} %get-tuple-element.13), kind=kLoop, calls=%fused_computation.12 | loop fusion | flops 12582912 | bytes 12599296 | tf_op jit(solution)/shard_map/convert_element_type | solution.py:130
  103.7 10.4 %all-to-all-start.1 = ((bf16[64,1,128,256]{3,2,1,0:T(8,128)(2,1)}), bf16[64,1,128,256]{3,2,1,0:T(8,128)(2,1)}, u32[]{:S(2)}, u32[]{:S(2)}) async-start(bf16[64,1,128,256]{3,2,1,0:T(8,128)(2,1)} %add_convert_fusion), calls=%async_computation.1 | async-start | bytes 8388608 | tf_op jit(solution)/shard_map/all_to_all | solution.py:131
  114.3 91.3 %all-to-all-done.1 = bf16[64,1,128,256]{3,2,1,0:T(8,128)(2,1)} async-done(((bf16[64,1,128,256]{3,2,1,0:T(8,128)(2,1)}), bf16[64,1,128,256]{3,2,1,0:T(8,128)(2,1)}, u32[]{:S(2)}, u32[]{:S(2)}) %all-to-all-start.1) | async-done | bytes 4194336 | tf_op jit(solution)/shard_map/all_to_all | solution.py:131
  205.6 2.8 gather_fusion.2
  210.5 2.2 slice_reduce_fusion
  214.0 10.0 %all-to-all-start.2 = ((bf16[64,1,128]{2,1,0:T(2,128)(2,1)}), bf16[64,1,128]{2,1,0:T(2,128)(2,1)S(1)}, u32[]{:S(2)}, u32[]{:S(2)}) async-start(bf16[64,1,128]{2,1,0:T(2,128)(2,1)} %copy.121), calls=%async_computation.2 | async-start | bytes 65536 | tf_op jit(solution)/shard_map/all_to_all | solution.py:132
  224.1 54.2 %all_gather.17 = bf16[256,1024]{0,1:T(8,128)(2,1)} all-gather(bf16[256,16]{0,1:T(8,128)(2,1)S(1)} %copy-done.10), channel_id=1, replica_groups=mesh['seq'=64,'tp'=4] {'seq'}, dimensions={1}, use_global_device_ids=true | all-gather | bytes 532480 | tf_op jit(solution)/shard_map/all_gather | solution.py:141
  281.0 3.1 fusion
  284.1 53.3 %all-gather.6.cloned.1.call-done = bf16[1024,3,256]{2,0,1:T(8,128)(2,1)} async-done(((bf16[16,3,256]{2,0,1:T(8,128)(2,1)}), bf16[1024,3,256]{2,0,1:T(8,128)(2,1)}) %all-gather.6.cloned.1.call-update) | async-done | bytes 1572880 | tf_op jit(solution)/shard_map/all_gather | solution.py:140
  337.4 7.9 %fusion.16 = bf16[16,128,3,256]{3,1,2,0:T(8,128)(2,1)} fusion(bf16[16,128,1024]{2,1,0:T(8,128)(2,1)} %all-gather.4.cloned.1.call-done, f32[1024]{0:T(1024)S(1)} %copy-done.12, f32[16,128]{1,0:T(8,128)S(1)} %add_rsqrt_fusion, bf16[1024,3,256]{2,0,1:T(8,128)(2,1)} %all-gather.6.cloned.1.call-done), kind=kOutput, calls=%fused_computation.28 | convolution fusion | flops 3231186944 | bytes 8925184 | tf_op jit(solution)/shard_map/une,eaf->unaf/dot_general | solution.py:32
  345.3 3.8 reshape.389
  349.0 3.2 fusion.69
  354.8 1.9 copy.150
  359.8 4.5 fusion.37
  364.4 84.3 %reduce-scatter.2.cloned.1.call-done = f32[512,1024]{1,0:T(8,128)} async-done(((f32[2048,1024]{1,0:T(8,128)}), f32[512,1024]{1,0:T(8,128)}) %reduce-scatter.2.cloned.1.call-update) | async-done | bytes 2097168 | tf_op jit(solution)/shard_map/reduce_scatter | solution.py:155
  448.7 3.2 add_convert_fusion.1
  452.3 43.8 %all_gather.19 = bf16[1024,2,128]{2,0,1:T(8,128)(2,1)S(1)} all-gather(bf16[16,2,128]{2,0,1:T(8,128)(2,1)S(1)} %copy.131), channel_id=1, replica_groups=mesh['seq'=64,'tp'=4] {'seq'}, dimensions={0}, use_global_device_ids=true | all-gather | bytes 532480 | tf_op jit(solution)/shard_map/all_gather | solution.py:169
  496.2 6.5 %all-gather.8.cloned.1.call-done = bf16[2048,1024]{1,0:T(8,128)(2,1)} async-done(((bf16[512,1024]{1,0:T(8,128)(2,1)}), bf16[2048,1024]{1,0:T(8,128)(2,1)}) %all-gather.8.cloned.1.call-update) | async-done | bytes 4194320 | tf_op jit(solution)/shard_map/all_gather | solution.py:168
  502.6 3.4 fusion.13
  506.1 1.9 collective-permute-start
  508.8 6.9 %collective-permute-done = bf16[256,2,128]{2,0,1:T(8,128)(2,1)S(1)} collective-permute-done((bf16[256,2,128]{2,0,1:T(8,128)(2,1)S(1)}, bf16[256,2,128]{2,0,1:T(8,128)(2,1)S(1)}, u32[]{:S(2)}, u32[]{:S(2)}) %collective-permute-start) | collective-permute-done | bytes 131104 | tf_op jit(solution)/shard_map/ppermute | solution.py:13
  (96 shorter events, 24.2 us)
Async XLA Ops:
  6.5 17.7 %copy-start = (s32[512,128]{1,0:T(8,128)S(1)}, s32[512,128]{1,0:T(8,128)}, u32[]{:S(2)}) copy-start(s32[512,128]{1,0:T(8,128)} %param.16) | copy-start | bytes 786436
  6.5 20.0 %copy-start.2 = (bf16[32,256]{1,0:T(8,128)(2,1)S(1)}, bf16[32,256]{1,0:T(8,128)(2,1)}, u32[]{:S(2)}) copy-start(bf16[32,256]{1,0:T(8,128)(2,1)} %param.22) | copy-start | bytes 49156
  103.7 101.9 %all-to-all-start.1 = ((bf16[64,1,128,256]{3,2,1,0:T(8,128)(2,1)}), bf16[64,1,128,256]{3,2,1,0:T(8,128)(2,1)}, u32[]{:S(2)}, u32[]{:S(2)}) async-start(bf16[64,1,128,256]{3,2,1,0:T(8,128)(2,1)} %add_convert_fusion), calls=%async_computation.1 | async-start | bytes 8388608 | tf_op jit(solution)/shard_map/all_to_all | solution.py:131
  114.1 96.3 %copy-start.6 = (bf16[512,2,256]{2,1,0:T(2,128)(2,1)S(1)}, bf16[512,2,256]{2,1,0:T(2,128)(2,1)}, u32[]{:S(2)}) copy-start(bf16[512,2,256]{2,1,0:T(2,128)(2,1)} %param.27) | copy-start | bytes 1572868
  114.1 98.5 %copy-start.9 = (s32[512,128]{1,0:T(8,128)S(1)}, s32[512,128]{1,0:T(8,128)}, u32[]{:S(2)}) copy-start(s32[512,128]{1,0:T(8,128)} %param.17) | copy-start | bytes 786436
  114.1 109.9 %copy-start.10 = (bf16[256,16]{0,1:T(8,128)(2,1)S(1)}, bf16[256,16]{0,1:T(8,128)(2,1)}, u32[]{:S(2)}) copy-start(bf16[256,16]{0,1:T(8,128)(2,1)} %param.26) | copy-start | bytes 24580
  114.2 166.8 %all-gather.4.cloned.1.call-start = ((), (), s32[]{:S(2)}) async-start(), calls=%async_computation.4 | async-start | bytes 5242880 | tf_op jit(solution)/shard_map/all_gather | solution.py:148
  205.6 73.5 %copy-start.13 = (f32[8]{0:T(128)S(1)}, f32[8]{0:T(128)}, u32[]{:S(2)}) copy-start(f32[8]{0:T(128)} %param.25) | copy-start | bytes 100
  209.6 127.8 %all-gather.6.cloned.1.call-start = ((), (), s32[]{:S(2)}) async-start(), calls=%async_computation.5 | async-start | bytes 1597440 | tf_op jit(solution)/shard_map/all_gather | solution.py:140
  210.4 126.9 %copy-start.12 = (f32[1024]{0:T(1024)S(1)}, f32[1024]{0:T(1024)}, u32[]{:S(2)}) copy-start(f32[1024]{0:T(1024)} %param.23) | copy-start | bytes 12292
  214.0 65.2 %all-to-all-start.2 = ((bf16[64,1,128]{2,1,0:T(2,128)(2,1)}), bf16[64,1,128]{2,1,0:T(2,128)(2,1)S(1)}, u32[]{:S(2)}, u32[]{:S(2)}) async-start(bf16[64,1,128]{2,1,0:T(2,128)(2,1)} %copy.121), calls=%async_computation.2 | async-start | bytes 65536 | tf_op jit(solution)/shard_map/all_to_all | solution.py:132
  224.0 224.7 %reduce-scatter.2.cloned.1.call-start = ((), (), s32[]{:S(2)}) async-start(), calls=%async_computation.6 | async-start | bytes 10485760 | tf_op jit(solution)/shard_map/reduce_scatter | solution.py:155
  349.0 3.7 copy-start.3
  353.6 1.2 copy-start.4
  354.8 3.7 copy-start.8
  356.8 3.0 copy-start.5
  364.3 87.6 %copy-start.11 = (bf16[16,2,128]{2,1,0:T(2,128)(2,1)S(1)}, bf16[16,2,128]{2,1,0:T(2,128)(2,1)}, u32[]{:S(2)}) copy-start(bf16[16,2,128]{2,1,0:T(2,128)(2,1)} %param.29) | copy-start | bytes 24580
  364.3 87.6 %copy-start.7 = (bf16[512,1024]{1,0:T(8,128)(2,1)S(1)}, bf16[512,1024]{1,0:T(8,128)(2,1)}, u32[]{:S(2)}) copy-start(bf16[512,1024]{1,0:T(8,128)(2,1)} %param.28) | copy-start | bytes 3145732
  364.4 138.2 %all-gather.8.cloned.1.call-start = ((), (), s32[]{:S(2)}) async-start(), calls=%async_computation.7 | async-start | bytes 5242880 | tf_op jit(solution)/shard_map/all_gather | solution.py:168
  448.7 47.4 %copy-start.14 = (s32[8]{0:T(128)S(1)}, s32[8]{0:T(128)}, u32[]{:S(2)}) copy-start(s32[8]{0:T(128)} %param.20) | copy-start | bytes 100
  506.1 9.6 %collective-permute-start = (bf16[256,2,128]{2,0,1:T(8,128)(2,1)S(1)}, bf16[256,2,128]{2,0,1:T(8,128)(2,1)S(1)}, u32[]{:S(2)}, u32[]{:S(2)}) collective-permute-start(bf16[256,2,128]{2,0,1:T(8,128)(2,1)S(1)} %slice.86), channel_id=1, source_target_pairs={{0,4},{4,8},{8,12},{12,16},{16,20},{20,24},{24,28},{28,32},{32,36}... | collective-permute-start | bytes 393224 | tf_op jit(solution)/shard_map/ppermute | solution.py:13
  518.0 4.0 copy-start.1
Sparse Core Ops, SparseCore 0:
  209.7 54.9 all-gather.3
  267.3 69.9 all-gather.5
  364.5 84.2 reduce-scatter.1
  452.1 50.4 all-gather.7
where the time goes:
time: 529 us
  waiting for transfers between devices  243 us (46%)
  blocking collectives  113 us (21%)
  local copies, waits for them, and re-layouts  91.8 us (17%)
  matrix products  22.6 us (4%)
  starting transfers between devices  22.5 us (4%)
  other arithmetic  21.9 us (4%)
  between operations  13.6 us (3%)
    all_to_all x1, waiting for transfers between devices, shards(): lax.all_to_all(embedded, 'seq', split_axis=0, concat_axis=0, tiled=True)  91.3 us
    reduce_scatter x1, waiting for transfers between devices, shards(): lax.psum_scatter(jnp.dot(mixed, row_out, preferred_element_type=jnp.float...  84.3 us
    all_gather x1, blocking collectives, shards(): lax.all_gather(enc_wo, 'seq', axis=1, tiled=True)  54.2 us
    all_gather x1, waiting for transfers between devices, shards(): lax.all_gather(enc_qkv, 'seq', axis=0, tiled=True)  53.3 us
    all_gather x1, blocking collectives, shards(): kv_weight = lax.all_gather(cca_kv, 'seq', axis=0, tiled=True)  43.8 us
    gather x1, local copies, waits for them, and re-layouts, shards(): jnp.take(table, tokens, axis=0).astype(jnp.float32)  35.5 us
    gather x1, local copies, waits for them, and re-layouts, shards(): jnp.take(depth_table, depths, axis=0).astype(jnp.float32)  33.1 us
    all_to_all x1, blocking collectives, shards(): lax.all_to_all(request, 'seq', split_axis=0, concat_axis=0, tiled=True)  15.1 us
  transfers between devices with their start and end apart: 7, of which 5 were waited for; matrix products, arithmetic and copies ran while one was open for 2% of the time, Pallas kernels for 0%

commit v1 on v0

--- a/solution.py
+++ b/solution.py
@@ -136,8 +136,20 @@
     parents = jnp.take(
         fetched_parents.reshape(seq_size * slot_count, length), target, axis=0
     ).astype(jnp.float32)
+
+    def steps_all_load(array_dim, which_axis, mine):
+        return jnp.concatenate(
+            lax.all_to_all(
+                jnp.stack([mine for _ in range(lax.axis_size(which_axis))]),
+                concat_axis=0,
+                split_axis=0,
+                axis_name=which_axis,
+            ),
+            axis=array_dim,
+        )
+
     row_qkv, row_out = (
-        lax.all_gather(enc_qkv, "seq", axis=0, tiled=True),
+        steps_all_load(0, "seq", enc_qkv),
         lax.all_gather(enc_wo, "seq", axis=1, tiled=True),
     )
     cond_columns = cond_kv.shape[2]

time: 529 us -> 512 us (0.968)
  waiting for transfers between devices: 243 us -> 188 us
  blocking collectives: 113 us -> 154 us
    all_gather x1 -> x0, waiting for transfers between devices: 53.3 us -> none  [shards(): lax.all_gather(enc_qkv, 'seq', axis=0, tiled=True)]
    all_gather x1, blocking collectives: 54.2 us -> 79.7 us  [shards(): lax.all_gather(enc_wo, 'seq', axis=1, tiled=True)]
    all_to_all x0 -> x1, blocking collectives: none -> 14.7 us  [shards(): lax.all_to_all(parents, 'seq', split_axis=0, concat_axis=0, tiled=True)]
  transfers between devices with their start and end apart: 7 -> 6, of which waited for: 5 -> 4; matrix products, arithmetic and copies ran while one was open for 2% -> 2% of each run, Pallas kernels for 0% -> 0%
where the time goes in v1:
time: 512 us
  waiting for transfers between devices  188 us (37%)
  blocking collectives  154 us (30%)
  local copies, waits for them, and re-layouts  92.5 us (18%)
  other arithmetic  22 us (4%)
  starting transfers between devices  21.9 us (4%)
  matrix products  19.7 us (4%)
  between operations  13.6 us (3%)
    all_to_all x1, waiting for transfers between devices, shards(): lax.all_to_all(embedded, 'seq', split_axis=0, concat_axis=0, tiled=True)  91.3 us
    reduce_scatter x1, waiting for transfers between devices, shards(): lax.psum_scatter(jnp.dot(mixed, row_out, preferred_element_type=jnp.float...  83.9 us
    all_gather x1, blocking collectives, shards(): lax.all_gather(enc_wo, 'seq', axis=1, tiled=True)  79.7 us
    all_gather x1, blocking collectives, shards(): kv_weight = lax.all_gather(cca_kv, 'seq', axis=0, tiled=True)  44 us
    gather x1, local copies, waits for them, and re-layouts, shards(): jnp.take(table, tokens, axis=0).astype(jnp.float32)  35.4 us
    gather x1, local copies, waits for them, and re-layouts, shards(): jnp.take(depth_table, depths, axis=0).astype(jnp.float32)  32.9 us
    all_to_all x1, blocking collectives, shards(): lax.all_to_all(request, 'seq', split_axis=0, concat_axis=0, tiled=True)  15.1 us
    all_to_all x1, blocking collectives, shards(): lax.all_to_all(parents, 'seq', split_axis=0, concat_axis=0, tiled=True)  14.7 us
  transfers between devices with their start and end apart: 6, of which 4 were waited for; matrix products, arithmetic and copies ran while one was open for 2% of the time, Pallas kernels for 0%

profile of v1, /device:TPU:128, one launch (start us, length us, event | category | flops | bytes accessed | tf_op | source)
XLA Modules:
  0.0 511.6 jit_solution(6799004804726428015)
XLA Ops:
  7.8 15.1 %all_to_all.27 = s32[64,1,1]{2,1,0:T(1,128)S(1)} all-to-all(s32[64,1,1]{2,1,0:T(1,128)S(1)} %copy.112), channel_id=1, replica_groups=mesh['seq'=64,'tp'=4] {'seq'}, dimensions={0} | all-to-all | bytes 512 | tf_op jit(solution)/shard_map/all_to_all | solution.py:123
  26.6 32.9 %gather_fusion.1 = bf16[8192,256]{1,0:T(8,128)(2,1)} fusion(bf16[32,256]{1,0:T(8,128)(2,1)S(1)} %copy-done.2, s32[8192]{0:T(1024)S(1)} %get-tuple-element.16), kind=kCustom, calls=%fused_computation.4 | custom fusion | bytes 8421376 | tf_op jit(solution)/shard_map/jit(_take)/gather | solution.py:129
  59.5 35.4 %gather_fusion = bf16[8192,256]{1,0:T(8,128)(2,1)} fusion(bf16[16384,256]{1,0:T(8,128)(2,1)} %param.21, s32[8192]{0:T(1024)S(1)} %get-tuple-element.15), kind=kCustom, calls=%fused_computation.3 | custom fusion | bytes 8421376 | tf_op jit(solution)/shard_map/jit(_take)/gather | solution.py:128
  94.9 8.5 %add_convert_fusion = bf16[64,1,128,256]{3,2,1,0:T(8,128)(2,1)} fusion(bf16[64,1,128,256]{3,2,1,0:T(8,128)(2,1)} %bitcast.205, bf16[64,1,128,256]{3,2,1,0:T(8,128)(2,1)} %bitcast.206, pred[64,128]{1,0:T(8,128)(4,1)S(1)} %get-tuple-element.14, pred[64,128]{1,0:T(8,128)(4,1)S(1)} %get-tuple-element.13), kind=kLoop, calls=%fused_computation.12 | loop fusion | flops 12582912 | bytes 12599296 | tf_op jit(solution)/shard_map/convert_element_type | solution.py:130
  103.4 10.4 %all-to-all-start.1 = ((bf16[64,1,128,256]{3,2,1,0:T(8,128)(2,1)}), bf16[64,1,128,256]{3,2,1,0:T(8,128)(2,1)}, u32[]{:S(2)}, u32[]{:S(2)}) async-start(bf16[64,1,128,256]{3,2,1,0:T(8,128)(2,1)} %add_convert_fusion), calls=%async_computation.1 | async-start | bytes 8388608 | tf_op jit(solution)/shard_map/all_to_all | solution.py:131
  114.0 91.3 %all-to-all-done.1 = bf16[64,1,128,256]{3,2,1,0:T(8,128)(2,1)} async-done(((bf16[64,1,128,256]{3,2,1,0:T(8,128)(2,1)}), bf16[64,1,128,256]{3,2,1,0:T(8,128)(2,1)}, u32[]{:S(2)}, u32[]{:S(2)}) %all-to-all-start.1) | async-done | bytes 4194336 | tf_op jit(solution)/shard_map/all_to_all | solution.py:131
  205.3 2.8 gather_fusion.2
  210.0 14.7 %all_to_all.28 = bf16[64,1,128]{2,1,0:T(2,128)(2,1)S(1)} all-to-all(bf16[64,1,128]{2,1,0:T(2,128)(2,1)S(1)} %copy.124), channel_id=1, replica_groups=mesh['seq'=64,'tp'=4] {'seq'}, dimensions={0} | all-to-all | bytes 32768 | tf_op jit(solution)/shard_map/all_to_all | solution.py:132
  225.9 9.5 %all-to-all-start.2 = ((bf16[64,16,3,256]{3,1,2,0:T(8,128)(2,1)}), bf16[64,16,3,256]{3,1,2,0:T(8,128)(2,1)S(1)}, u32[]{:S(2)}, u32[]{:S(2)}) async-start(bf16[64,16,3,256]{3,1,2,0:T(8,128)(2,1)} %stack.2), calls=%async_computation.2 | async-start | bytes 3145728 | tf_op jit(solution)/shard_map/all_to_all | solution.py:142
  235.5 2.2 slice_reduce_fusion
  238.6 79.7 %all_gather.13 = bf16[256,1024]{0,1:T(8,128)(2,1)} all-gather(bf16[256,16]{0,1:T(8,128)(2,1)S(1)} %copy-done.12), channel_id=1, replica_groups=mesh['seq'=64,'tp'=4] {'seq'}, dimensions={1}, use_global_device_ids=true | all-gather | bytes 532480 | tf_op jit(solution)/shard_map/all_gather | solution.py:153
  320.4 3.2 fusion
  323.8 4.9 fusion.16
  328.7 3.8 reshape.395
  332.5 3.2 fusion.68
  338.3 1.9 copy.153
  343.3 4.5 fusion.36
  347.9 83.9 %reduce-scatter.2.cloned.1.call-done = f32[512,1024]{1,0:T(8,128)} async-done(((f32[2048,1024]{1,0:T(8,128)}), f32[512,1024]{1,0:T(8,128)}) %reduce-scatter.2.cloned.1.call-update) | async-done | bytes 2097168 | tf_op jit(solution)/shard_map/reduce_scatter | solution.py:167
  431.8 3.2 add_convert_fusion.1
  435.4 44.0 %all_gather.15 = bf16[1024,2,128]{2,0,1:T(8,128)(2,1)S(1)} all-gather(bf16[16,2,128]{2,0,1:T(8,128)(2,1)S(1)} %copy.134), channel_id=1, replica_groups=mesh['seq'=64,'tp'=4] {'seq'}, dimensions={0}, use_global_device_ids=true | all-gather | bytes 532480 | tf_op jit(solution)/shard_map/all_gather | solution.py:181
  479.4 6.2 %all-gather.5.cloned.1.call-done = bf16[2048,1024]{1,0:T(8,128)(2,1)} async-done(((bf16[512,1024]{1,0:T(8,128)(2,1)}), bf16[2048,1024]{1,0:T(8,128)(2,1)}) %all-gather.5.cloned.1.call-update) | async-done | bytes 4194320 | tf_op jit(solution)/shard_map/all_gather | solution.py:180
  485.6 3.4 fusion.13
  489.2 1.9 collective-permute-start
  491.9 6.9 %collective-permute-done = bf16[256,2,128]{2,0,1:T(8,128)(2,1)S(1)} collective-permute-done((bf16[256,2,128]{2,0,1:T(8,128)(2,1)S(1)}, bf16[256,2,128]{2,0,1:T(8,128)(2,1)S(1)}, u32[]{:S(2)}, u32[]{:S(2)}) %collective-permute-start) | collective-permute-done | bytes 131104 | tf_op jit(solution)/shard_map/ppermute | solution.py:13
  (100 shorter events, 24.4 us)
Async XLA Ops:
  6.5 17.7 %copy-start = (s32[512,128]{1,0:T(8,128)S(1)}, s32[512,128]{1,0:T(8,128)}, u32[]{:S(2)}) copy-start(s32[512,128]{1,0:T(8,128)} %param.16) | copy-start | bytes 786436
  6.5 20.0 %copy-start.2 = (bf16[32,256]{1,0:T(8,128)(2,1)S(1)}, bf16[32,256]{1,0:T(8,128)(2,1)}, u32[]{:S(2)}) copy-start(bf16[32,256]{1,0:T(8,128)(2,1)} %param.22) | copy-start | bytes 49156
  103.4 101.9 %all-to-all-start.1 = ((bf16[64,1,128,256]{3,2,1,0:T(8,128)(2,1)}), bf16[64,1,128,256]{3,2,1,0:T(8,128)(2,1)}, u32[]{:S(2)}, u32[]{:S(2)}) async-start(bf16[64,1,128,256]{3,2,1,0:T(8,128)(2,1)} %add_convert_fusion), calls=%async_computation.1 | async-start | bytes 8388608 | tf_op jit(solution)/shard_map/all_to_all | solution.py:131
  113.8 95.5 %copy-start.10 = (s32[512,128]{1,0:T(8,128)S(1)}, s32[512,128]{1,0:T(8,128)}, u32[]{:S(2)}) copy-start(s32[512,128]{1,0:T(8,128)} %param.17) | copy-start | bytes 786436
  113.8 110.9 %copy-start.11 = (bf16[16,3,256]{2,0,1:T(8,128)(2,1)S(1)}, bf16[16,3,256]{2,0,1:T(8,128)(2,1)}, u32[]{:S(2)}) copy-start(bf16[16,3,256]{2,0,1:T(8,128)(2,1)} %param.24) | copy-start | bytes 73732
  113.8 206.5 %all-gather.3.cloned.1.call-start = ((), (), s32[]{:S(2)}) async-start(), calls=%async_computation.5 | async-start | bytes 5242880 | tf_op jit(solution)/shard_map/all_gather | solution.py:160
  208.1 27.4 %copy-start.7 = (bf16[512,2,256]{2,1,0:T(2,128)(2,1)S(1)}, bf16[512,2,256]{2,1,0:T(2,128)(2,1)}, u32[]{:S(2)}) copy-start(bf16[512,2,256]{2,1,0:T(2,128)(2,1)} %param.27) | copy-start | bytes 1572868
  209.2 29.3 %copy-start.15 = (f32[8]{0:T(128)S(1)}, f32[8]{0:T(128)}, u32[]{:S(2)}) copy-start(f32[8]{0:T(128)} %param.25) | copy-start | bytes 100
  209.2 29.4 %copy-start.12 = (bf16[256,16]{0,1:T(8,128)(2,1)S(1)}, bf16[256,16]{0,1:T(8,128)(2,1)}, u32[]{:S(2)}) copy-start(bf16[256,16]{0,1:T(8,128)(2,1)} %param.26) | copy-start | bytes 24580
  225.9 94.2 %all-to-all-start.2 = ((bf16[64,16,3,256]{3,1,2,0:T(8,128)(2,1)}), bf16[64,16,3,256]{3,1,2,0:T(8,128)(2,1)S(1)}, u32[]{:S(2)}, u32[]{:S(2)}) async-start(bf16[64,16,3,256]{3,1,2,0:T(8,128)(2,1)} %stack.2), calls=%async_computation.2 | async-start | bytes 3145728 | tf_op jit(solution)/shard_map/all_to_all | solution.py:142
  235.4 196.4 %reduce-scatter.2.cloned.1.call-start = ((), (), s32[]{:S(2)}) async-start(), calls=%async_computation.6 | async-start | bytes 10485760 | tf_op jit(solution)/shard_map/reduce_scatter | solution.py:167
  319.1 4.6 copy-start.14
  320.4 3.5 copy-start.3
  332.5 3.7 copy-start.4
  337.1 1.2 copy-start.5
  338.2 3.7 copy-start.9
  340.2 3.0 copy-start.6
  347.8 87.2 %copy-start.13 = (bf16[16,2,128]{2,1,0:T(2,128)(2,1)S(1)}, bf16[16,2,128]{2,1,0:T(2,128)(2,1)}, u32[]{:S(2)}) copy-start(bf16[16,2,128]{2,1,0:T(2,128)(2,1)} %param.29) | copy-start | bytes 24580
  347.8 87.2 %copy-start.8 = (bf16[512,1024]{1,0:T(8,128)(2,1)S(1)}, bf16[512,1024]{1,0:T(8,128)(2,1)}, u32[]{:S(2)}) copy-start(bf16[512,1024]{1,0:T(8,128)(2,1)} %param.28) | copy-start | bytes 3145732
  347.8 137.8 %all-gather.5.cloned.1.call-start = ((), (), s32[]{:S(2)}) async-start(), calls=%async_computation.7 | async-start | bytes 5242880 | tf_op jit(solution)/shard_map/all_gather | solution.py:180
  431.8 47.6 %copy-start.16 = (s32[8]{0:T(128)S(1)}, s32[8]{0:T(128)}, u32[]{:S(2)}) copy-start(s32[8]{0:T(128)} %param.20) | copy-start | bytes 100
  489.2 9.6 %collective-permute-start = (bf16[256,2,128]{2,0,1:T(8,128)(2,1)S(1)}, bf16[256,2,128]{2,0,1:T(8,128)(2,1)S(1)}, u32[]{:S(2)}, u32[]{:S(2)}) collective-permute-start(bf16[256,2,128]{2,0,1:T(8,128)(2,1)S(1)} %slice.86), channel_id=1, source_target_pairs={{0,4},{4,8},{8,12},{12,16},{16,20},{20,24},{24,28},{28,32},{32,36}... | collective-permute-start | bytes 393224 | tf_op jit(solution)/shard_map/ppermute | solution.py:13
  501.0 4.1 copy-start.1
Sparse Core Ops, SparseCore 0:
  209.4 54.9 all-gather.2
  347.9 83.8 reduce-scatter.1
  435.1 50.4 all-gather.4
